TPU v7x, 768 devices: a whole 4x8x12 slice. The times are simulated.
768 devices in a mesh: gx: 64 (over z_lo, y, core), gy: 12 (over x, z_hi).
Axes of the slice: x: 4, y: 8, z: 12 (z_hi: 3, z_lo: 4; z = z_hi * 4 + z_lo), core: 2. Of those that a mesh axis runs over, the one named last changes fastest.
Arguments:
- load: float32 [64, 12, 96, 896], P('gx', 'gy'), may hold values from -80 to 80
- dual_operator: bfloat16 [64, 12, 896, 896], P('gx', 'gy'), may hold values from -1 to 2
- dirichlet: bfloat16 [64, 12, 896, 896], P('gx', 'gy'), may hold values from -1 to 2
- modes: bfloat16 [64, 12, 12, 896], P('gx', 'gy'), may hold values from -1 to 1
- coarse_inverse: float32 [64, 144, 12, 768], P('gx', None, 'gy'), may hold values from -1 to 2, as said below
- face_counts: int32 [64, 12, 4], P('gx', 'gy'), may hold values from 0 to 224, as said below
- partners: int32 [64, 12, 4, 224], P('gx', 'gy'), may hold values from 0 to 223, as said below
Outputs:
- multipliers: float32 [64, 12, 96, 896], P('gx', 'gy')
- residual: float32 [64, 12, 96, 896], P('gx', 'gy')
Inputs may be any that keep to these rules, and one draw needn't show every extreme that they name: `face_counts`: the two faces of one interface have equal counts; faces on the grid's outer boundary have 0; every other face has at least half of 224; some face has exactly 224. `partners`: each face's list is a permutation of the slots that maps the live slots onto the live slots of the neighbour's facing face; the facing face's list is its inverse. `coarse_inverse`: the coarse inverse is symmetric: the entry of coefficients u, v equals that of v, u.
All inputs are finite; a program needn't handle non-finite values.
Results may differ from a plain program's by a relative error of at most 0.00365.
The roundings to bfloat16 on the way count: a program that leaves them out, or rounds other values in their place, can miss the bound.
Values may be sent and summed in bfloat16 or wider, within the bound.
A program may use at most 64 MiB of HBM per device.

v0:
```python
import jax
import jax.numpy as jnp
from jax import lax
from jax.sharding import PartitionSpec as P

precise = lax.Precision.HIGHEST
spectrum_low = 0.5
spectrum_high = 4.0


def extended(shard, sides, width):
    for axis, dim in sides:
        size, length = (lax.axis_size(axis), shard.shape[dim])
        up = [(i, (i + 1) % size) for i in range(size - 1)]
        down = [(j, i) for i, j in up]
        last = lax.slice_in_dim(shard, length - width, length, axis=dim)
        first = lax.slice_in_dim(shard, 0, width, axis=dim)
        before = lax.ppermute(last, axis, up)
        after = lax.ppermute(first, axis, down)
        shard = jnp.concatenate([before, shard, after], axis=dim)
    return shard


def chebyshev_coefficients():
    center = (spectrum_high + spectrum_low) / 2.0
    radius = (spectrum_high - spectrum_low) / 2.0
    center_ratio = center / radius
    factor_prev = 1.0 / center_ratio
    result = [(1.0 / center, 0.0)]
    factor = 1.0 / (2.0 * center_ratio - factor_prev)
    result.append((2.0 * factor / radius, factor * factor_prev))
    return result


def assemble_west_east(values, partner_slots):
    face_width = partner_slots.shape[1]
    shaped = values.reshape(values.shape[0], 2, face_width)
    padded = extended(shaped, (("gx", 1),), 1)
    west_sum = values[:, :face_width] + jnp.take(padded[:, 0], partner_slots[0], axis=1)
    east_sum = values[:, face_width:] + jnp.take(padded[:, 3], partner_slots[1], axis=1)
    return (west_sum, east_sum)


def assemble_south_north(values, partner_slots):
    face_width = partner_slots.shape[1]
    shaped = values.reshape(values.shape[0], 2, face_width)
    padded = extended(shaped, (("gy", 1),), 1)
    south_sum = values[:, :face_width] + jnp.take(padded[:, 0], partner_slots[2], axis=1)
    north_sum = values[:, face_width:] + jnp.take(padded[:, 3], partner_slots[3], axis=1)
    return (south_sum, north_sum)


def assemble(values, partner_slots, live_slots):
    split_at = values.shape[1] // 2
    west_sum, east_sum = assemble_west_east(values[:, :split_at], partner_slots)
    south_sum, north_sum = assemble_south_north(values[:, split_at:], partner_slots)
    return jnp.concatenate([west_sum, east_sum, south_sum, north_sum], axis=1) * live_slots


def apply_block(vector, matrix, partner_slots, live_slots):
    rounded = vector.astype(jnp.bfloat16)
    split_at = matrix.shape[1] // 2
    product = jnp.dot(rounded, matrix, preferred_element_type=jnp.float32)
    west_sum, east_sum = assemble_west_east(product[:, :split_at], partner_slots)
    south_sum, north_sum = assemble_south_north(product[:, split_at:], partner_slots)
    return jnp.concatenate([west_sum, east_sum, south_sum, north_sum], axis=1) * live_slots


def coarse_values(coeffs, inverse_block):
    partial_terms = lax.dot_general(
        lax.all_gather(coeffs, "gx", axis=1, tiled=True),
        inverse_block,
        (((1,), (1,)), ((), ())),
        precision=precise,
        preferred_element_type=jnp.float32,
    )
    return lax.psum_scatter(partial_terms, "gy", scatter_dimension=1, tiled=True)


def project(vector, mode_rows, inverse_block, partner_slots, live_slots):
    coeffs = jnp.dot(vector, mode_rows.T, precision=precise, preferred_element_type=jnp.float32)
    solved = coarse_values(coeffs, inverse_block)
    own_part = jnp.dot(solved, mode_rows, precision=precise, preferred_element_type=jnp.float32)
    correction = assemble(own_part, partner_slots, live_slots)
    return vector - correction


def local(load, dual_operator, dirichlet, modes, coarse_inverse, face_counts, partners):
    partner_slots = partners[0, 0]
    face_width = partner_slots.shape[1]
    positions = lax.broadcasted_iota(jnp.int32, (4, face_width), 1)
    live_slots = (
        (positions < face_counts[0, 0][:, None]).astype(jnp.float32).reshape(1, 4 * face_width)
    )
    mode_half = modes[0, 0]
    mode_rows = mode_half.astype(jnp.float32)
    inverse_block = coarse_inverse[0, :, 0, :]
    dual_local = dual_operator[0, 0]
    dirichlet_local = dirichlet[0, 0]
    chebyshev = chebyshev_coefficients()
    gap_values = assemble(load[0, 0], partner_slots, live_slots)
    residual = project(gap_values, mode_rows, inverse_block, partner_slots, live_slots)
    multipliers = jnp.zeros_like(residual)
    direction = jnp.zeros_like(residual)
    for alpha_step, beta_step in chebyshev:
        smoothed = apply_block(residual, dirichlet_local, partner_slots, live_slots)
        preconditioned = project(smoothed, mode_rows, inverse_block, partner_slots, live_slots)
        direction = alpha_step * preconditioned + beta_step * direction
        multipliers = multipliers + direction
        applied = apply_block(direction, dual_local, partner_slots, live_slots)
        residual = residual - project(applied, mode_rows, inverse_block, partner_slots, live_slots)
    return (multipliers[None, None], residual[None, None])


def solution(mesh):
    return jax.shard_map(
        local,
        mesh=mesh,
        in_specs=(
            P("gx", "gy", None, None),
            P("gx", "gy", None, None),
            P("gx", "gy", None, None),
            P("gx", "gy", None, None),
            P("gx", None, "gy", None),
            P("gx", "gy", None),
            P("gx", "gy", None, None),
        ),
        out_specs=(P("gx", "gy", None, None), P("gx", "gy", None, None)),
        check_vma=False,
    )
```

profile of v0, /device:TPU:1, one launch (start us, length us, event | category | flops | bytes accessed | tf_op | source)
XLA Modules:
  0.0 1009.2 jit_solution(8811918934287732786)
XLA Ops:
  2.1 4.6 collective-permute-start
  6.7 9.1 collective-permute-start.1
  15.9 3.5 collective-permute-start.2
  25.6 5.5 collective-permute-done.3
  32.5 86.0 %all-gather = f32[64,12,96]{2,1,0:T(8,128)S(1)} all-gather(f32[1,12,96]{2,1,0:T(8,128)S(1)} %convolution_bitcast_fusion.4), channel_id=1, replica_groups=mesh['gx'=64,'gy'=12] {'gx'}, dimensions={0}, use_global_device_ids=true | all-gather | bytes 299520 | tf_op jit(solution)/shard_map/all_gather | solution.py:71
  119.3 64.1 %all-reduce = f32[96,144]{1,0:T(8,128)S(1)} all-reduce(f32[96,144]{1,0:T(8,128)S(1)} %fusion.16), channel_id=2, replica_groups=mesh['gx'=64,'gy'=12] {'gy'}, use_global_device_ids=true, to_apply=%region_0.0.clone | all-reduce | flops 13824 | bytes 110592
  184.7 10.1 %collective-permute-start.4 = (f32[96,1,224]{0,2,1:T(8,128)}, f32[96,1,224]{0,2,1:T(8,128)S(1)}, u32[]{:S(2)}, u32[]{:S(2)}) collective-permute-start(f32[96,1,224]{0,2,1:T(8,128)} %get-tuple-element.95), channel_id=1, source_target_pairs={{0,12},{12,24},{24,36},{36,48},{48,60},{60,72},{72,84},{84,96},{96... | collective-permute-start | bytes 258056 | tf_op jit(solution)/shard_map/ppermute | solution.py:18
  194.8 3.8 collective-permute-start.5
  205.3 6.8 collective-permute-done.7
  216.8 2.4 collective-permute-start.9
  220.0 5.5 collective-permute-start.10
  229.8 6.8 collective-permute-done.11
  238.8 78.0 %all-gather.1 = f32[64,12,96]{2,1,0:T(8,128)S(1)} all-gather(f32[1,12,96]{2,1,0:T(8,128)S(1)} %convolution_bitcast_fusion.3), channel_id=1, replica_groups=mesh['gx'=64,'gy'=12] {'gx'}, dimensions={0}, use_global_device_ids=true | all-gather | bytes 299520 | tf_op jit(solution)/shard_map/all_gather | solution.py:71
  317.7 60.7 %all-reduce.1 = f32[96,144]{1,0:T(8,128)S(1)} all-reduce(f32[96,144]{1,0:T(8,128)S(1)} %fusion.14), channel_id=3, replica_groups=mesh['gx'=64,'gy'=12] {'gy'}, use_global_device_ids=true, to_apply=%region_1.3.clone | all-reduce | flops 13824 | bytes 110592
  379.7 12.0 %collective-permute-start.12 = (f32[96,1,224]{0,2,1:T(8,128)}, f32[96,1,224]{0,2,1:T(8,128)S(1)}, u32[]{:S(2)}, u32[]{:S(2)}) collective-permute-start(f32[96,1,224]{0,2,1:T(8,128)} %get-tuple-element.87), channel_id=1, source_target_pairs={{0,12},{12,24},{24,36},{36,48},{48,60},{60,72},{72,84},{84,96},{96... | collective-permute-start | bytes 258056 | tf_op jit(solution)/shard_map/ppermute | solution.py:18
  391.7 2.2 collective-permute-start.13
  394.8 3.4 collective-permute-start.14
  402.6 6.7 collective-permute-done.15
  411.2 2.1 fusion.2
  414.3 3.1 collective-permute-start.16
  420.2 4.2 collective-permute-start.18
  428.6 5.9 collective-permute-done.19
  436.7 78.1 %all-gather.2 = f32[64,12,96]{2,1,0:T(8,128)S(1)} all-gather(f32[1,12,96]{2,1,0:T(8,128)S(1)} %convolution_bitcast_fusion.2), channel_id=1, replica_groups=mesh['gx'=64,'gy'=12] {'gx'}, dimensions={0}, use_global_device_ids=true | all-gather | bytes 299520 | tf_op jit(solution)/shard_map/all_gather | solution.py:71
  515.7 62.7 %all-reduce.2 = f32[96,144]{1,0:T(8,128)S(1)} all-reduce(f32[96,144]{1,0:T(8,128)S(1)} %fusion.12), channel_id=4, replica_groups=mesh['gx'=64,'gy'=12] {'gy'}, use_global_device_ids=true, to_apply=%region_2.4.clone | all-reduce | flops 13824 | bytes 110592
  579.7 10.8 %collective-permute-start.20 = (f32[96,1,224]{0,2,1:T(8,128)}, f32[96,1,224]{0,2,1:T(8,128)S(1)}, u32[]{:S(2)}, u32[]{:S(2)}) collective-permute-start(f32[96,1,224]{0,2,1:T(8,128)} %get-tuple-element.79), channel_id=1, source_target_pairs={{0,12},{12,24},{24,36},{36,48},{48,60},{60,72},{72,84},{84,96},{96... | collective-permute-start | bytes 258056 | tf_op jit(solution)/shard_map/ppermute | solution.py:18
  590.5 2.8 collective-permute-start.21
  594.1 2.0 collective-permute-start.22
  602.3 4.8 collective-permute-done.23
  612.6 2.6 collective-permute-start.24
  618.0 5.4 collective-permute-start.26
  627.6 6.5 collective-permute-done.27
  636.4 78.6 %all-gather.3 = f32[64,12,96]{2,1,0:T(8,128)S(1)} all-gather(f32[1,12,96]{2,1,0:T(8,128)S(1)} %convolution_bitcast_fusion.1), channel_id=1, replica_groups=mesh['gx'=64,'gy'=12] {'gx'}, dimensions={0}, use_global_device_ids=true | all-gather | bytes 299520 | tf_op jit(solution)/shard_map/all_gather | solution.py:71
  715.9 60.6 %all-reduce.3 = f32[96,144]{1,0:T(8,128)S(1)} all-reduce(f32[96,144]{1,0:T(8,128)S(1)} %fusion.10), channel_id=5, replica_groups=mesh['gx'=64,'gy'=12] {'gy'}, use_global_device_ids=true, to_apply=%region_3.5.clone | all-reduce | flops 13824 | bytes 110592
  777.7 11.3 %collective-permute-start.28 = (f32[96,1,224]{0,2,1:T(8,128)}, f32[96,1,224]{0,2,1:T(8,128)S(1)}, u32[]{:S(2)}, u32[]{:S(2)}) collective-permute-start(f32[96,1,224]{0,2,1:T(8,128)} %get-tuple-element.71), channel_id=1, source_target_pairs={{0,12},{12,24},{24,36},{36,48},{48,60},{60,72},{72,84},{84,96},{96... | collective-permute-start | bytes 258056 | tf_op jit(solution)/shard_map/ppermute | solution.py:18
  789.0 2.8 collective-permute-start.29
  792.7 3.5 collective-permute-start.30
  800.5 6.7 collective-permute-done.31
  809.1 2.7 fusion
  812.7 3.1 collective-permute-start.32
  818.7 3.7 collective-permute-start.34
  826.8 5.9 collective-permute-done.35
  834.8 78.2 %all-gather.4 = f32[64,12,96]{2,1,0:T(8,128)S(1)} all-gather(f32[1,12,96]{2,1,0:T(8,128)S(1)} %convolution_bitcast_fusion), channel_id=1, replica_groups=mesh['gx'=64,'gy'=12] {'gx'}, dimensions={0}, use_global_device_ids=true | all-gather | bytes 299520 | tf_op jit(solution)/shard_map/all_gather | solution.py:71
  913.8 62.9 %all-reduce.4 = f32[96,144]{1,0:T(8,128)S(1)} all-reduce(f32[96,144]{1,0:T(8,128)S(1)} %fusion.8), channel_id=6, replica_groups=mesh['gx'=64,'gy'=12] {'gy'}, use_global_device_ids=true, to_apply=%region_4.6.clone | all-reduce | flops 13824 | bytes 110592
  978.1 10.7 %collective-permute-start.36 = (f32[96,1,224]{0,2,1:T(8,128)}, f32[96,1,224]{0,2,1:T(8,128)S(1)}, u32[]{:S(2)}, u32[]{:S(2)}) collective-permute-start(f32[96,1,224]{0,2,1:T(8,128)} %get-tuple-element.63), channel_id=1, source_target_pairs={{0,12},{12,24},{24,36},{36,48},{48,60},{60,72},{72,84},{84,96},{96... | collective-permute-start | bytes 258056 | tf_op jit(solution)/shard_map/ppermute | solution.py:18
  988.7 3.4 collective-permute-start.37
  995.7 2.6 fusion.27
  1001.3 4.1 collective-permute-done.39
  1006.5 2.7 fusion.30
  (428 shorter events, 99.4 us)
Async XLA Ops:
  0.6 212.7 %copy-start = (bf16[1,1,896,896]{3,2,1,0:T(8,128)(2,1)S(1)}, bf16[1,1,896,896]{3,2,1,0:T(8,128)(2,1)}, u32[]{:S(2)}) copy-start(bf16[1,1,896,896]{3,2,1,0:T(8,128)(2,1)} %param.11) | copy-start | bytes 4816900
  0.6 20.1 %copy-start.101 = (s32[1,1,4,224]{3,2,1,0:T(4,128)S(1)}, s32[1,1,4,224]{3,2,1,0:T(4,128)}, u32[]{:S(2)}) copy-start(s32[1,1,4,224]{3,2,1,0:T(4,128)} %param.15) | copy-start | bytes 10756
  0.7 20.2 %copy-start.102 = (s32[1,1,4]{2,1,0:T(1,128)S(1)}, s32[1,1,4]{2,1,0:T(1,128)}, u32[]{:S(2)}) copy-start(s32[1,1,4]{2,1,0:T(1,128)} %param.14) | copy-start | bytes 52
  2.1 21.0 %collective-permute-start = (f32[96,1,224]{0,2,1:T(8,128)S(1)}, f32[96,1,224]{0,2,1:T(8,128)S(1)}, u32[]{:S(2)}, u32[]{:S(2)}) collective-permute-start(f32[96,1,224]{0,2,1:T(8,128)S(1)} %get-tuple-element.99), channel_id=1, source_target_pairs={{0,12},{12,24},{24,36},{36,48},{48,60},{60,72},{72,84},{84,96},{96... | collective-permute-start | bytes 258056 | tf_op jit(solution)/shard_map/ppermute | solution.py:18
  6.7 17.2 %collective-permute-start.1 = (f32[96,1,224]{0,2,1:T(8,128)S(1)}, f32[96,1,224]{0,2,1:T(8,128)S(1)}, u32[]{:S(2)}, u32[]{:S(2)}) collective-permute-start(f32[96,1,224]{0,2,1:T(8,128)S(1)} %get-tuple-element.100), channel_id=1, source_target_pairs={{12,0},{24,12},{36,24},{48,36},{60,48},{72,60},{84,72},{96,84},{10... | collective-permute-start | bytes 258056 | tf_op jit(solution)/shard_map/ppermute | solution.py:19
  15.9 8.8 collective-permute-start.2
  19.4 11.6 %collective-permute-start.3 = (f32[96,1,224]{0,2,1:T(8,128)S(1)}, f32[96,1,224]{0,2,1:T(8,128)S(1)}, u32[]{:S(2)}, u32[]{:S(2)}) collective-permute-start(f32[96,1,224]{0,2,1:T(8,128)S(1)} %get-tuple-element.102), channel_id=1, source_target_pairs={{1,0},{2,1},{3,2},{4,3},{5,4},{6,5},{7,6},{8,7},{9,8},{10,9},{11,1... | collective-permute-start | bytes 258056 | tf_op jit(solution)/shard_map/ppermute | solution.py:19
  20.8 11.1 %copy-start.66 = (pred[224]{0:T(512)(128)(4,1)}, pred[224]{0:T(512)(128)(4,1)S(1)}, u32[]{:S(2)}) copy-start(pred[224]{0:T(512)(128)(4,1)S(1)} %get-tuple-element.109) | copy-start | bytes 676
  31.9 86.6 %copy-start.1 = (f32[1,144,1,768]{3,2,1,0:T(1,128)S(1)}, f32[1,144,1,768]{3,2,1,0:T(1,128)}, u32[]{:S(2)}) copy-start(f32[1,144,1,768]{3,2,1,0:T(1,128)} %param.13) | copy-start | bytes 1327108
  184.7 17.7 %collective-permute-start.4 = (f32[96,1,224]{0,2,1:T(8,128)}, f32[96,1,224]{0,2,1:T(8,128)S(1)}, u32[]{:S(2)}, u32[]{:S(2)}) collective-permute-start(f32[96,1,224]{0,2,1:T(8,128)} %get-tuple-element.95), channel_id=1, source_target_pairs={{0,12},{12,24},{24,36},{36,48},{48,60},{60,72},{72,84},{84,96},{96... | collective-permute-start | bytes 258056 | tf_op jit(solution)/shard_map/ppermute | solution.py:18
  194.8 8.5 collective-permute-start.5
  199.4 4.9 collective-permute-start.6
  201.1 11.1 %collective-permute-start.7 = (f32[96,1,224]{0,2,1:T(8,128)}, f32[96,1,224]{0,2,1:T(8,128)S(1)}, u32[]{:S(2)}, u32[]{:S(2)}) collective-permute-start(f32[96,1,224]{0,2,1:T(8,128)} %get-tuple-element.98), channel_id=1, source_target_pairs={{1,0},{2,1},{3,2},{4,3},{5,4},{6,5},{7,6},{8,7},{9,8},{10,9},{11,1... | collective-permute-start | bytes 258056 | tf_op jit(solution)/shard_map/ppermute | solution.py:19
  214.9 12.0 %collective-permute-start.8 = (f32[96,1,224]{0,2,1:T(8,128)}, f32[96,1,224]{0,2,1:T(8,128)S(1)}, u32[]{:S(2)}, u32[]{:S(2)}) collective-permute-start(f32[96,1,224]{0,2,1:T(8,128)} %get-tuple-element.91), channel_id=1, source_target_pairs={{0,12},{12,24},{24,36},{36,48},{48,60},{60,72},{72,84},{84,96},{96... | collective-permute-start | bytes 258056 | tf_op jit(solution)/shard_map/ppermute | solution.py:18
  216.8 11.0 %collective-permute-start.9 = (f32[96,1,224]{0,2,1:T(8,128)}, f32[96,1,224]{0,2,1:T(8,128)S(1)}, u32[]{:S(2)}, u32[]{:S(2)}) collective-permute-start(f32[96,1,224]{0,2,1:T(8,128)} %get-tuple-element.92), channel_id=1, source_target_pairs={{12,0},{24,12},{36,24},{48,36},{60,48},{72,60},{84,72},{96,84},{10... | collective-permute-start | bytes 258056 | tf_op jit(solution)/shard_map/ppermute | solution.py:19
  220.0 8.8 collective-permute-start.10
  225.6 11.1 %collective-permute-start.11 = (f32[96,1,224]{0,2,1:T(8,128)}, f32[96,1,224]{0,2,1:T(8,128)S(1)}, u32[]{:S(2)}, u32[]{:S(2)}) collective-permute-start(f32[96,1,224]{0,2,1:T(8,128)} %get-tuple-element.94), channel_id=1, source_target_pairs={{1,0},{2,1},{3,2},{4,3},{5,4},{6,5},{7,6},{8,7},{9,8},{10,9},{11,1... | collective-permute-start | bytes 258056 | tf_op jit(solution)/shard_map/ppermute | solution.py:19
  379.7 19.8 %collective-permute-start.12 = (f32[96,1,224]{0,2,1:T(8,128)}, f32[96,1,224]{0,2,1:T(8,128)S(1)}, u32[]{:S(2)}, u32[]{:S(2)}) collective-permute-start(f32[96,1,224]{0,2,1:T(8,128)} %get-tuple-element.87), channel_id=1, source_target_pairs={{0,12},{12,24},{24,36},{36,48},{48,60},{60,72},{72,84},{84,96},{96... | collective-permute-start | bytes 258056 | tf_op jit(solution)/shard_map/ppermute | solution.py:18
  391.7 8.7 collective-permute-start.13
  394.8 6.7 collective-permute-start.14
  398.2 11.1 %collective-permute-start.15 = (f32[96,1,224]{0,2,1:T(8,128)}, f32[96,1,224]{0,2,1:T(8,128)S(1)}, u32[]{:S(2)}, u32[]{:S(2)}) collective-permute-start(f32[96,1,224]{0,2,1:T(8,128)} %get-tuple-element.90), channel_id=1, source_target_pairs={{1,0},{2,1},{3,2},{4,3},{5,4},{6,5},{7,6},{8,7},{9,8},{10,9},{11,1... | collective-permute-start | bytes 258056 | tf_op jit(solution)/shard_map/ppermute | solution.py:19
  414.3 11.4 %collective-permute-start.16 = (f32[96,1,224]{0,2,1:T(8,128)}, f32[96,1,224]{0,2,1:T(8,128)S(1)}, u32[]{:S(2)}, u32[]{:S(2)}) collective-permute-start(f32[96,1,224]{0,2,1:T(8,128)} %get-tuple-element.83), channel_id=1, source_target_pairs={{0,12},{12,24},{24,36},{36,48},{48,60},{60,72},{72,84},{84,96},{96... | collective-permute-start | bytes 258056 | tf_op jit(solution)/shard_map/ppermute | solution.py:18
  417.4 9.2 collective-permute-start.17
  420.2 7.5 collective-permute-start.18
  424.4 10.2 %collective-permute-start.19 = (f32[96,1,224]{0,2,1:T(8,128)}, f32[96,1,224]{0,2,1:T(8,128)S(1)}, u32[]{:S(2)}, u32[]{:S(2)}) collective-permute-start(f32[96,1,224]{0,2,1:T(8,128)} %get-tuple-element.86), channel_id=1, source_target_pairs={{1,0},{2,1},{3,2},{4,3},{5,4},{6,5},{7,6},{8,7},{9,8},{10,9},{11,1... | collective-permute-start | bytes 258056 | tf_op jit(solution)/shard_map/ppermute | solution.py:19
  579.7 17.7 %collective-permute-start.20 = (f32[96,1,224]{0,2,1:T(8,128)}, f32[96,1,224]{0,2,1:T(8,128)S(1)}, u32[]{:S(2)}, u32[]{:S(2)}) collective-permute-start(f32[96,1,224]{0,2,1:T(8,128)} %get-tuple-element.79), channel_id=1, source_target_pairs={{0,12},{12,24},{24,36},{36,48},{48,60},{60,72},{72,84},{84,96},{96... | collective-permute-start | bytes 258056 | tf_op jit(solution)/shard_map/ppermute | solution.py:18
  590.5 8.4 collective-permute-start.21
  594.1 6.4 collective-permute-start.22
  596.1 11.1 %collective-permute-start.23 = (f32[96,1,224]{0,2,1:T(8,128)}, f32[96,1,224]{0,2,1:T(8,128)S(1)}, u32[]{:S(2)}, u32[]{:S(2)}) collective-permute-start(f32[96,1,224]{0,2,1:T(8,128)} %get-tuple-element.82), channel_id=1, source_target_pairs={{1,0},{2,1},{3,2},{4,3},{5,4},{6,5},{7,6},{8,7},{9,8},{10,9},{11,1... | collective-permute-start | bytes 258056 | tf_op jit(solution)/shard_map/ppermute | solution.py:19
  612.6 12.0 %collective-permute-start.24 = (f32[96,1,224]{0,2,1:T(8,128)}, f32[96,1,224]{0,2,1:T(8,128)S(1)}, u32[]{:S(2)}, u32[]{:S(2)}) collective-permute-start(f32[96,1,224]{0,2,1:T(8,128)} %get-tuple-element.75), channel_id=1, source_target_pairs={{0,12},{12,24},{24,36},{36,48},{48,60},{60,72},{72,84},{84,96},{96... | collective-permute-start | bytes 258056 | tf_op jit(solution)/shard_map/ppermute | solution.py:18
  615.2 10.4 %collective-permute-start.25 = (f32[96,1,224]{0,2,1:T(8,128)}, f32[96,1,224]{0,2,1:T(8,128)S(1)}, u32[]{:S(2)}, u32[]{:S(2)}) collective-permute-start(f32[96,1,224]{0,2,1:T(8,128)} %get-tuple-element.76), channel_id=1, source_target_pairs={{12,0},{24,12},{36,24},{48,36},{60,48},{72,60},{84,72},{96,84},{10... | collective-permute-start | bytes 258056 | tf_op jit(solution)/shard_map/ppermute | solution.py:19
  618.0 8.6 collective-permute-start.26
  623.4 10.8 %collective-permute-start.27 = (f32[96,1,224]{0,2,1:T(8,128)}, f32[96,1,224]{0,2,1:T(8,128)S(1)}, u32[]{:S(2)}, u32[]{:S(2)}) collective-permute-start(f32[96,1,224]{0,2,1:T(8,128)} %get-tuple-element.78), channel_id=1, source_target_pairs={{1,0},{2,1},{3,2},{4,3},{5,4},{6,5},{7,6},{8,7},{9,8},{10,9},{11,1... | collective-permute-start | bytes 258056 | tf_op jit(solution)/shard_map/ppermute | solution.py:19
  777.7 19.7 %collective-permute-start.28 = (f32[96,1,224]{0,2,1:T(8,128)}, f32[96,1,224]{0,2,1:T(8,128)S(1)}, u32[]{:S(2)}, u32[]{:S(2)}) collective-permute-start(f32[96,1,224]{0,2,1:T(8,128)} %get-tuple-element.71), channel_id=1, source_target_pairs={{0,12},{12,24},{24,36},{36,48},{48,60},{60,72},{72,84},{84,96},{96... | collective-permute-start | bytes 258056 | tf_op jit(solution)/shard_map/ppermute | solution.py:18
  789.0 9.4 collective-permute-start.29
  792.7 6.7 collective-permute-start.30
  796.1 11.1 %collective-permute-start.31 = (f32[96,1,224]{0,2,1:T(8,128)}, f32[96,1,224]{0,2,1:T(8,128)S(1)}, u32[]{:S(2)}, u32[]{:S(2)}) collective-permute-start(f32[96,1,224]{0,2,1:T(8,128)} %get-tuple-element.74), channel_id=1, source_target_pairs={{1,0},{2,1},{3,2},{4,3},{5,4},{6,5},{7,6},{8,7},{9,8},{10,9},{11,1... | collective-permute-start | bytes 258056 | tf_op jit(solution)/shard_map/ppermute | solution.py:19
  812.7 11.1 %collective-permute-start.32 = (f32[96,1,224]{0,2,1:T(8,128)}, f32[96,1,224]{0,2,1:T(8,128)S(1)}, u32[]{:S(2)}, u32[]{:S(2)}) collective-permute-start(f32[96,1,224]{0,2,1:T(8,128)} %get-tuple-element.67), channel_id=1, source_target_pairs={{0,12},{12,24},{24,36},{36,48},{48,60},{60,72},{72,84},{84,96},{96... | collective-permute-start | bytes 258056 | tf_op jit(solution)/shard_map/ppermute | solution.py:18
  815.9 8.9 collective-permute-start.33
  818.7 7.2 collective-permute-start.34
  822.3 10.4 %collective-permute-start.35 = (f32[96,1,224]{0,2,1:T(8,128)}, f32[96,1,224]{0,2,1:T(8,128)S(1)}, u32[]{:S(2)}, u32[]{:S(2)}) collective-permute-start(f32[96,1,224]{0,2,1:T(8,128)} %get-tuple-element.70), channel_id=1, source_target_pairs={{1,0},{2,1},{3,2},{4,3},{5,4},{6,5},{7,6},{8,7},{9,8},{10,9},{11,1... | collective-permute-start | bytes 258056 | tf_op jit(solution)/shard_map/ppermute | solution.py:19
  913.8 81.9 %copy-start.23 = (f32[96,224]{1,0:T(8,128)S(1)}, f32[96,224]{1,0:T(8,128)}, u32[]{:S(2)}) copy-start(f32[96,224]{1,0:T(8,128)} %copy-done.20) | copy-start | bytes 258052
  913.8 81.9 %copy-start.27 = (f32[96,224]{1,0:T(8,128)S(1)}, f32[96,224]{1,0:T(8,128)}, u32[]{:S(2)}) copy-start(f32[96,224]{1,0:T(8,128)} %copy-done.24) | copy-start | bytes 258052
  913.8 81.9 %copy-start.29 = (f32[96,224]{1,0:T(8,128)S(1)}, f32[96,224]{1,0:T(8,128)}, u32[]{:S(2)}) copy-start(f32[96,224]{1,0:T(8,128)} %copy-done.28) | copy-start | bytes 258052
  978.1 20.2 %collective-permute-start.36 = (f32[96,1,224]{0,2,1:T(8,128)}, f32[96,1,224]{0,2,1:T(8,128)S(1)}, u32[]{:S(2)}, u32[]{:S(2)}) collective-permute-start(f32[96,1,224]{0,2,1:T(8,128)} %get-tuple-element.63), channel_id=1, source_target_pairs={{0,12},{12,24},{24,36},{36,48},{48,60},{60,72},{72,84},{84,96},{96... | collective-permute-start | bytes 258056 | tf_op jit(solution)/shard_map/ppermute | solution.py:18
  988.7 10.5 %collective-permute-start.37 = (f32[96,1,224]{0,2,1:T(8,128)}, f32[96,1,224]{0,2,1:T(8,128)S(1)}, u32[]{:S(2)}, u32[]{:S(2)}) collective-permute-start(f32[96,1,224]{0,2,1:T(8,128)} %get-tuple-element.64), channel_id=1, source_target_pairs={{12,0},{24,12},{36,24},{48,36},{60,48},{72,60},{84,72},{96,84},{10... | collective-permute-start | bytes 258056 | tf_op jit(solution)/shard_map/ppermute | solution.py:19
  993.0 7.2 collective-permute-start.38
  994.4 11.1 %collective-permute-start.39 = (f32[96,1,224]{0,2,1:T(8,128)}, f32[96,1,224]{0,2,1:T(8,128)S(1)}, u32[]{:S(2)}, u32[]{:S(2)}) collective-permute-start(f32[96,1,224]{0,2,1:T(8,128)} %get-tuple-element.66), channel_id=1, source_target_pairs={{1,0},{2,1},{3,2},{4,3},{5,4},{6,5},{7,6},{8,7},{9,8},{10,9},{11,1... | collective-permute-start | bytes 258056 | tf_op jit(solution)/shard_map/ppermute | solution.py:19
  (95 other events, 599.4 us)
where the time goes:
time: 1010 us
  blocking collectives  710 us (70%)
  starting transfers between devices  150 us (15%)
  local copies, waits for them, and re-layouts  61.7 us (6%)
  waiting for transfers between devices  59.9 us (6%)
  matrix products  14.6 us (1%)
    all_gather x5, blocking collectives, coarse_values(): lax.all_gather(coeffs, 'gx', axis=1, tiled=True)  399 us
    unnamed x5, blocking collectives  311 us
    ppermute x20, starting transfers between devices, extended(): before = lax.ppermute(last, axis, up)  104 us
    ppermute x20, waiting for transfers between devices, extended(): after = lax.ppermute(first, axis, down)  59.8 us
    ppermute x20, starting transfers between devices, extended(): after = lax.ppermute(first, axis, down)  45.4 us
  transfers between devices with their start and end apart: 40, of which 10 were waited for; matrix products, arithmetic and copies ran while one was open for 4% of the time, Pallas kernels for 0%

commit v1 on v0

v1 whole, which is shorter than its diff:
```python
import functools

import jax
import jax.numpy as jnp
from jax import lax
from jax.experimental import pallas as pl
from jax.experimental.pallas import tpu as pltpu
from jax.sharding import PartitionSpec as P

MESH = pl.DeviceIdType.MESH
F32 = jnp.float32
BF16 = jnp.bfloat16
ROUNDS = 5
spectrum_low = 0.5
spectrum_high = 4.0


def chebyshev_coefficients():
    center = (spectrum_high + spectrum_low) / 2.0
    radius = (spectrum_high - spectrum_low) / 2.0
    center_ratio = center / radius
    factor_prev = 1.0 / center_ratio
    result = [(1.0 / center, 0.0)]
    factor = 1.0 / (2.0 * center_ratio - factor_prev)
    result.append((2.0 * factor / radius, factor * factor_prev))
    return result


def halves(x):
    high = x.astype(BF16)
    return high, (x - high.astype(F32)).astype(BF16)


def thirds(x):
    high = x.astype(BF16)
    rest = x - high.astype(F32)
    mid = rest.astype(BF16)
    return high, mid, (rest - mid.astype(F32)).astype(BF16)


def mm(a, b):
    return jnp.dot(a, b, preferred_element_type=F32)


def dot_nt(a, b):
    return lax.dot_general(a, b, (((1,), (1,)), ((), ())), preferred_element_type=F32)


def dot_tn(a, b):
    return lax.dot_general(a, b, (((0,), (0,)), ((), ())), preferred_element_type=F32)


def kernel(
    nx, ny,
    slot_ref, load_ref, modes_ref, dual_hbm, dirichlet_hbm, inverse_hbm,
    mult_ref, res_ref,
    weights, inverse_raw, pick, mode_ext, mode_send, mode_recv,
    y_ref, v_ref, dir_ref, inv_high, inv_low,
    face_send, face_recv, part_send, part_recv, gathered,
    partial, scattered, solved_send, solved_recv,
    local_sem, mode_ssem, mode_rsem, face_ssem, face_rsem, part_ssem, part_rsem,
    gather_ssem, gather_rsem, relay_ssem, relay_rsem,
    scatter_ssem, scatter_rsem, solved_ssem, solved_rsem,
):
    loads, slots = load_ref.shape
    modes = modes_ref.shape[0]
    face = slots // 4
    face_pad = face_send.shape[2]
    padded = gathered.shape[3]
    lanes = gathered.shape[4]
    chips = nx // 2
    a = lax.axis_index("gx")
    b = lax.axis_index("gy")
    core = lax.rem(a, 2)
    chip = lax.div(a, 2)
    partner = a + 1 - 2 * core
    exists = (a > 0, a < nx - 1, b > 0, b < ny - 1)
    neighbours = ((a - 1, b), (a + 1, b), (a, b - 1), (a, b + 1))

    def remote(src, dst, ssem, rsem, device):
        return pltpu.make_async_remote_copy(
            src_ref=src, dst_ref=dst, send_sem=ssem, recv_sem=rsem,
            device_id=device, device_id_type=MESH)

    copies = (
        pltpu.make_async_copy(inverse_hbm, inverse_raw, local_sem.at[0]),
        pltpu.make_async_copy(dirichlet_hbm, weights.at[0], local_sem.at[1]),
        pltpu.make_async_copy(dual_hbm, weights.at[1], local_sem.at[2]),
    )
    for c in copies:
        c.start()

    barrier = pltpu.get_barrier_semaphore()

    def greet(device):
        pl.semaphore_signal(barrier, inc=1, device_id=device, device_id_type=MESH)

    @pl.loop(1, chips)
    def _(i):
        greet((2 * lax.rem(chip + i, chips) + core, b))

    @pl.loop(1, ny)
    def _(i):
        greet((a, lax.rem(b + i, ny)))

    for f in (0, 1):
        @pl.when(exists[f])
        def _(f=f):
            greet(neighbours[f])

    wide = modes_ref[...].astype(F32)
    mode_send[...] = jnp.zeros_like(mode_send)
    for f in range(4):
        mode_send[f, 0:modes, 0:face] = wide[:, f * face:(f + 1) * face]
    face_send[...] = jnp.zeros_like(face_send)
    part_send[...] = jnp.zeros_like(part_send)
    slot = slot_ref[...]
    live = (slot >= 0).astype(F32)
    for f in range(4):
        rows = lax.broadcasted_iota(jnp.int32, (face_pad, slots), 0) + f * face_pad
        pick[f] = (rows == slot).astype(F32).astype(BF16)
    own_modes = jnp.concatenate([wide * live, jnp.zeros((padded - modes, slots), F32)], axis=0)
    mode_ext[0:padded, :] = own_modes.astype(BF16)
    y_ref[...] = load_ref[...]

    pl.semaphore_wait(
        barrier, chips - 1 + ny - 1 + (a > 0).astype(jnp.int32) + (a < nx - 1).astype(jnp.int32))

    def mode_copy(f, g):
        return remote(mode_send.at[f], mode_recv.at[g], mode_ssem.at[f], mode_rsem.at[g], neighbours[f])

    for f in range(4):
        @pl.when(exists[f])
        def _(f=f):
            mode_copy(f, f ^ 1).start()

    copies[0].wait()
    raw_high, raw_low = halves(inverse_raw[...])
    out_row = lax.broadcasted_iota(jnp.int32, (ny * padded, ny * modes), 0)
    in_row = lax.broadcasted_iota(jnp.int32, (ny * padded, ny * modes), 1)
    place = lax.bitwise_and(out_row, padded - 1)
    row_pick = ((lax.shift_right_logical(out_row, 4) * modes + place == in_row) & (place < modes))
    row_pick = row_pick.astype(F32).astype(BF16)
    raw_high = mm(row_pick, raw_high).astype(BF16)
    raw_low = mm(row_pick, raw_low).astype(BF16)
    for p in range(2):
        in_col = lax.broadcasted_iota(jnp.int32, (nx * modes, chips * padded), 0)
        out_col = lax.broadcasted_iota(jnp.int32, (nx * modes, chips * padded), 1)
        place = lax.bitwise_and(out_col, padded - 1)
        source = (2 * lax.shift_right_logical(out_col, 4) + p) * modes + place
        col_pick = ((source == in_col) & (place < modes)).astype(F32).astype(BF16)
        inv_high[p] = mm(raw_high, col_pick).astype(BF16)
        inv_low[p] = mm(raw_low, col_pick).astype(BF16)
    copies[1].wait()
    copies[2].wait()

    for f in range(4):
        @pl.when(exists[f])
        def _(f=f):
            mode_copy(f, f).wait_recv()
        given = jnp.where(exists[f], mode_recv[f], 0.0).astype(BF16)
        mode_ext[(f + 1) * padded:(f + 2) * padded, :] = mm(given, pick[f]).astype(BF16)

    for f in range(4):
        @pl.when(exists[f])
        def _(f=f):
            mode_copy(f, f ^ 1).wait_send()

    used_row = lax.broadcasted_iota(jnp.int32, (padded, lanes), 0) < modes
    chebyshev = chebyshev_coefficients()

    def body(r, carry):
        def part_copy(f, g):
            return remote(part_send.at[f + 1, 0:modes], part_recv.at[r, g, 0:modes],
                          part_ssem.at[f], part_rsem.at[r, g], neighbours[f])

        def face_copy(f, g):
            return remote(face_send.at[f], face_recv.at[r, g],
                          face_ssem.at[f], face_rsem.at[r, g], neighbours[f])

        def solved_copy(f, g):
            return remote(solved_send.at[0:modes], solved_recv.at[r, g, 0:modes],
                          solved_ssem.at[f], solved_rsem.at[r, g], neighbours[f])

        def gather_copy(block, device):
            return remote(block, block, gather_ssem, gather_rsem.at[r], device)

        def relay_copy(p):
            block = gathered.at[r, p, :, 0:modes]
            return remote(block, block, relay_ssem, relay_rsem.at[r], (partner, b))

        def scatter_copy(src, dst, device):
            return remote(src, dst, scatter_ssem, scatter_rsem.at[r], device)

        y = y_ref[...]
        y_high, y_low = halves(y)
        parts = dot_nt(mode_ext[...], y_high) + dot_nt(mode_ext[...], y_low)
        for f in range(5):
            part_send[f, :, 0:loads] = parts[f * padded:(f + 1) * padded]
        for f in range(4):
            @pl.when(exists[f])
            def _(f=f):
                part_copy(f, f ^ 1).start()
        for f in range(4):
            face_send[f, :, 0:face] = y[:, f * face:(f + 1) * face]

        coeffs = part_send[0]
        for f in range(4):
            @pl.when(exists[f])
            def _(f=f):
                part_copy(f, f).wait_recv()
            coeffs = coeffs + jnp.where(exists[f], part_recv[r, f], 0.0)
        gathered[r, core, chip] = coeffs

        @pl.loop(1, chips)
        def _(i):
            gather_copy(gathered.at[r, core, chip, 0:modes],
                        (2 * lax.rem(chip + i, chips) + core, b)).start()

        for f in range(4):
            @pl.when(exists[f])
            def _(f=f):
                face_copy(f, f ^ 1).start()

        others = gathered.at[r, core, 0:chips - 1, 0:modes]
        gather_copy(others, (partner, b)).wait_recv()
        relay_copy(core).start()

        def coarse(p):
            values = jnp.where(used_row[None], gathered[r, p], 0.0).reshape(chips * padded, lanes)
            high, low = halves(values)
            return mm(inv_high[p], high) + mm(inv_high[p], low) + mm(inv_low[p], high)

        half = coarse(core)
        relay_copy(1 - core).wait_recv()
        partial[...] = (half + coarse(1 - core)).reshape(ny, padded, lanes)

        @pl.loop(1, ny)
        def _(i):
            other = lax.rem(b + i, ny)
            scatter_copy(partial.at[other, 0:modes], scattered.at[r, b, 0:modes], (a, other)).start()

        matched = live * y
        for f in range(4):
            @pl.when(exists[f])
            def _(f=f):
                face_copy(f, f).wait_recv()
            for piece in thirds(jnp.where(exists[f], face_recv[r, f], 0.0)):
                matched = matched + mm(piece, pick[f])
        v_ref[...] = matched

        scatter_copy(partial.at[0:ny - 1, 0:modes], scattered.at[r, 0:ny - 1, 0:modes], (partner, b)).wait_recv()
        solved = jnp.where(b == 0, partial[0], scattered[r, 0])
        for e in range(1, ny):
            solved = solved + jnp.where(b == e, partial[e], scattered[r, e])
        solved_send[...] = solved
        for f in range(4):
            @pl.when(exists[f])
            def _(f=f):
                solved_copy(f, f ^ 1).start()

        blocks = [jnp.where(used_row, solved, 0.0)]
        for f in range(4):
            @pl.when(exists[f])
            def _(f=f):
                solved_copy(f, f).wait_recv()
            blocks.append(jnp.where(used_row & exists[f], solved_recv[r, f], 0.0))
        high, low = halves(jnp.concatenate(blocks, axis=0))
        correction = dot_tn(high, mode_ext[...]) + dot_tn(low, mode_ext[...])
        out = v_ref[...] - correction[0:loads]

        for f in range(4):
            @pl.when(exists[f])
            def _(f=f):
                part_copy(f, f ^ 1).wait_send()
                face_copy(f, f ^ 1).wait_send()
                solved_copy(f, f ^ 1).wait_send()
        gather_copy(others, (partner, b)).wait_send()
        relay_copy(core).wait_send()
        scatter_copy(partial.at[0:ny - 1, 0:modes], scattered.at[r, 0:ny - 1, 0:modes], (partner, b)).wait_send()

        def advance(vector, which):
            y_ref[...] = mm(vector.astype(BF16), weights[which])

        @pl.when(r == 0)
        def _():
            res_ref[...] = out
            advance(out, 0)

        @pl.when(r == 1)
        def _():
            step = chebyshev[0][0] * out
            dir_ref[...] = step
            mult_ref[...] = step
            advance(step, 1)

        @pl.when(r == 2)
        def _():
            rest = res_ref[...] - out
            res_ref[...] = rest
            advance(rest, 0)

        @pl.when(r == 3)
        def _():
            step = chebyshev[1][0] * out + chebyshev[1][1] * dir_ref[...]
            mult_ref[...] = mult_ref[...] + step
            advance(step, 1)

        @pl.when(r == 4)
        def _():
            res_ref[...] = res_ref[...] - out

        return carry

    lax.fori_loop(0, ROUNDS, body, 0)


def local(nx, ny, load, dual_operator, dirichlet, modes, coarse_inverse, face_counts, partners):
    loads, slots = load.shape[2:]
    count = modes.shape[2]
    face = slots // 4
    face_pad = -(-face // 128) * 128
    padded = 16
    lanes = 128
    positions = lax.broadcasted_iota(jnp.int32, (4, face), 1)
    base = lax.broadcasted_iota(jnp.int32, (4, face), 0) * face_pad
    slot = jnp.where(positions < face_counts[0, 0][:, None], partners[0, 0] + base, -1)
    slot = slot.reshape(1, slots)
    vmem = pl.BlockSpec(memory_space=pltpu.VMEM)
    hbm = pl.BlockSpec(memory_space=pl.ANY)
    dma = pltpu.SemaphoreType.DMA
    multipliers, residual = pl.pallas_call(
        functools.partial(kernel, nx, ny),
        out_shape=(jax.ShapeDtypeStruct((loads, slots), F32),) * 2,
        in_specs=[vmem, vmem, vmem, hbm, hbm, hbm],
        out_specs=(vmem, vmem),
        scratch_shapes=[
            pltpu.VMEM((2, slots, slots), BF16),
            pltpu.VMEM((ny * count, nx * count), F32),
            pltpu.VMEM((4, face_pad, slots), BF16),
            pltpu.VMEM((5 * padded, slots), BF16),
            pltpu.VMEM((4, padded, face_pad), F32),
            pltpu.VMEM((4, padded, face_pad), F32),
            pltpu.VMEM((loads, slots), F32),
            pltpu.VMEM((loads, slots), F32),
            pltpu.VMEM((loads, slots), F32),
            pltpu.VMEM((2, ny * padded, nx // 2 * padded), BF16),
            pltpu.VMEM((2, ny * padded, nx // 2 * padded), BF16),
            pltpu.VMEM((4, loads, face_pad), F32),
            pltpu.VMEM((ROUNDS, 4, loads, face_pad), F32),
            pltpu.VMEM((5, padded, lanes), F32),
            pltpu.VMEM((ROUNDS, 4, padded, lanes), F32),
            pltpu.VMEM((ROUNDS, 2, nx // 2, padded, lanes), F32),
            pltpu.VMEM((ny, padded, lanes), F32),
            pltpu.VMEM((ROUNDS, ny, padded, lanes), F32),
            pltpu.VMEM((padded, lanes), F32),
            pltpu.VMEM((ROUNDS, 4, padded, lanes), F32),
            dma((3,)), dma((4,)), dma((4,)), dma((4,)), dma((ROUNDS, 4)),
            dma((4,)), dma((ROUNDS, 4)), dma, dma((ROUNDS,)), dma, dma((ROUNDS,)),
            dma, dma((ROUNDS,)), dma((4,)), dma((ROUNDS, 4)),
        ],
        compiler_params=pltpu.CompilerParams(
            collective_id=0, has_side_effects=True, vmem_limit_bytes=56 * 1024 * 1024),
    )(slot, load[0, 0], modes[0, 0], dual_operator[0, 0], dirichlet[0, 0], coarse_inverse[0, :, 0, :])
    return multipliers[None, None], residual[None, None]


def solution(mesh):
    nx, ny = mesh.shape["gx"], mesh.shape["gy"]
    return jax.shard_map(
        functools.partial(local, nx, ny),
        mesh=mesh,
        in_specs=(
            P("gx", "gy", None, None),
            P("gx", "gy", None, None),
            P("gx", "gy", None, None),
            P("gx", "gy", None, None),
            P("gx", None, "gy", None),
            P("gx", "gy", None),
            P("gx", "gy", None, None),
        ),
        out_specs=(P("gx", "gy", None, None), P("gx", "gy", None, None)),
        check_vma=False,
    )
```

time: 1010 us -> 188 us (0.19)
  blocking collectives: 710 us -> 0 us
  Pallas kernels: 0 us -> 178 us
  starting transfers between devices: 150 us -> 0 us
  waiting for transfers between devices: 59.9 us -> 0 us
  local copies, waits for them, and re-layouts: 61.7 us -> 6.29 us
  matrix products: 14.6 us -> 0 us
    all_gather x5 -> x0, blocking collectives: 399 us -> none  [coarse_values(): lax.all_gather(coeffs, 'gx', axis=1, tiled=True)]
    unnamed x5 -> x0, blocking collectives: 311 us -> none
    pallas_call x0 -> x1, Pallas kernels: none -> 178 us  [local(): pl.pallas_call(functools.partial(kernel, nx, ny), out_shape=(jax.ShapeDty...]
    ppermute x40 -> x0, starting transfers between devices: 150 us -> none  [the longest x20 104 us: extended(): before = lax.ppermute(last, axis, up)]
    ppermute x40 -> x0, waiting for transfers between devices: 59.9 us -> none  [the longest x20 59.8 us: extended(): after = lax.ppermute(first, axis, down)]
    gather x80 -> x0, local copies, waits for them, and re-layouts: 39.2 us -> none  [the longest x20 10.4 us: assemble_south_north(): jnp.take(padded[:, 0], partner_slots[2], axis=1)]
    slice x31 -> x0, local copies, waits for them, and re-layouts: 15 us -> none  [the longest x20 12.8 us: extended(): last = lax.slice_in_dim(shard, length - width, length, axis=dim)]
    dot_general x19 -> x0, matrix products: 14.6 us -> none  [the longest x4 7.08 us: apply_block(): product = jnp.dot(rounded, matrix, preferred_element_type=jnp.float32)]
  transfers between devices with their start and end apart: 40 -> 0, of which waited for: 10 -> 0; matrix products, arithmetic and copies ran while one was open for 4% -> 0% of each run, Pallas kernels for 0% -> 0%
where the time goes in v1:
time: 188 us; the launch traced here: 186 us
  Pallas kernels  178 us (95%)
  local copies, waits for them, and re-layouts  6.29 us (3%)
    pallas_call x1, Pallas kernels, local(): pl.pallas_call(functools.partial(kernel, nx, ny), out_shape=(jax.ShapeDty...  178 us
    unnamed x3, local copies, waits for them, and re-layouts  5.27 us

profile of v1, /device:TPU:1, one launch (start us, length us, event | category | flops | bytes accessed | tf_op | source)
XLA Modules:
  0.0 186.0 jit_solution(17202467737235968420)
XLA Ops:
  0.6 0.7 iota_compare_fusion
  1.4 0.1 lt.23
  1.5 0.1 iota.17
  1.5 0.1 iota.18
  1.6 0.8 squeeze.18
  2.4 0.6 add_select_fusion.slot_ref
  3.0 1.8 copy.11
  4.8 177.7 %shard_map.86 = (f32[96,896]{1,0:T(8,128)}, f32[96,896]{1,0:T(8,128)}) custom-call(s32[1,896]{1,0:T(1,128)} %add_select_fusion.slot_ref, f32[96,896]{1,0:T(8,128)} %bitcast.15, bf16[12,896]{1,0:T(8,128)(2,1)} %bitcast.16, bf16[896,896]{1,0:T(8,128)(2,1)} %bitcast.11, bf16[896,896]{1,0:T(8,128)(2,1)} %bitcast.12, f32[144,768]{1,0:T(8,128)} %bitcast.10), custom_call_target="tpu_custom_call" | custom-call | tf_op jit(solution)/shard_map/pallas_call | solution.py:332
  182.5 1.7 copy.14
  184.2 1.7 copy.15
  (1 shorter events, 0.0 us)

commit v2 on v1

v2 whole, which is shorter than its diff:
```python
import functools

import jax
import jax.numpy as jnp
from jax import lax
from jax.experimental import pallas as pl
from jax.experimental.pallas import tpu as pltpu
from jax.sharding import PartitionSpec as P

MESH = pl.DeviceIdType.MESH
F32 = jnp.float32
BF16 = jnp.bfloat16
ROUNDS = 5
spectrum_low = 0.5
spectrum_high = 4.0


def chebyshev_coefficients():
    center = (spectrum_high + spectrum_low) / 2.0
    radius = (spectrum_high - spectrum_low) / 2.0
    center_ratio = center / radius
    factor_prev = 1.0 / center_ratio
    result = [(1.0 / center, 0.0)]
    factor = 1.0 / (2.0 * center_ratio - factor_prev)
    result.append((2.0 * factor / radius, factor * factor_prev))
    return result


def halves(x):
    high = x.astype(BF16)
    return high, (x - high.astype(F32)).astype(BF16)


def thirds(x):
    high = x.astype(BF16)
    rest = x - high.astype(F32)
    mid = rest.astype(BF16)
    return high, mid, (rest - mid.astype(F32)).astype(BF16)


def wrap_rows(x, loads, rows):
    spare = x.shape[1] - loads
    row = lax.bitwise_and(lax.broadcasted_iota(jnp.int32, x.shape, 0), 15)
    lane = lax.broadcasted_iota(jnp.int32, x.shape, 1)
    out = x
    for j in range(3):
        moved = pltpu.roll(pltpu.roll(x, loads - spare * j, 1), x.shape[0] - rows + 3 * j, 0)
        out = jnp.where((lane >= loads) & (row >= 3 * j) & (row < 3 * j + 3), moved, out)
    return out


def unwrap_rows(x, loads, rows):
    spare = x.shape[1] - loads
    row = lax.bitwise_and(lax.broadcasted_iota(jnp.int32, x.shape, 0), 15)
    lane = lax.broadcasted_iota(jnp.int32, x.shape, 1)
    out = jnp.where((row < rows) & (lane < loads), x, 0.0)
    for j in range(3):
        moved = pltpu.roll(pltpu.roll(x, spare * (j + 1), 1), rows - 3 * j, 0)
        here = (row >= rows) & (row < rows + 3) & (lane >= spare * j) & (lane < spare * (j + 1))
        out = jnp.where(here, moved, out)
    return out


def mm(a, b):
    return jnp.dot(a, b, preferred_element_type=F32)


def dot_nt(a, b):
    return lax.dot_general(a, b, (((1,), (1,)), ((), ())), preferred_element_type=F32)


def dot_tn(a, b):
    return lax.dot_general(a, b, (((0,), (0,)), ((), ())), preferred_element_type=F32)


def kernel(
    nx, ny,
    counts_hbm, partners_hbm, load_hbm, modes_hbm, dual_hbm, dirichlet_hbm, inverse_hbm,
    mult_ref, step_ref, res_ref, last_ref,
    counts_ref, partners_ref, modes_ref, x_ref, dm_high, dm_low,
    weights, inverse_raw, pick, mode_ext, mode_send, mode_recv,
    y_ref, v_ref, inv_high, inv_low,
    face_send, face_recv, part_send, near_recv, gathered,
    partial, across_recv, summed, along_recv, side_recv,
    local_sem, mode_ssem, mode_rsem, face_ssem, face_rsem, near_ssem, near_rsem,
    gather_ssem, gather_rsem, relay_ssem, relay_rsem,
    across_ssem, across_rsem, along_ssem, along_rsem, side_ssem, side_rsem,
):
    loads, slots = y_ref.shape
    modes = modes_ref.shape[0]
    face = slots // 4
    face_pad = face_send.shape[2]
    padded, lanes = gathered.shape[4:]
    depth = gathered.shape[2] + 1
    width = gathered.shape[3]
    height = along_recv.shape[1]
    length = ny // height
    chips = nx // 2
    a = lax.axis_index("gx")
    b = lax.axis_index("gy")
    core = lax.rem(a, 2)
    chip = lax.div(a, 2)
    layer = lax.div(chip, width)
    column = lax.rem(chip, width)
    far = lax.div(b, height)
    rise = lax.rem(b, height)

    def seat(z, y, c):
        return 2 * (z * width + y) + c

    next_column = (lax.rem(column + width - 1 + core, width), lax.rem(column + core, width))
    steps = sorted(range(1, width), key=lambda i: -min(i, width - i))
    partner = a + 1 - 2 * core
    exists = (a > 0, a < nx - 1, b > 0, b < ny - 1)
    neighbours = ((a - 1, b), (a + 1, b), (a, b - 1), (a, b + 1))

    def remote(src, dst, ssem, rsem, device):
        return pltpu.make_async_remote_copy(
            src_ref=src, dst_ref=dst, send_sem=ssem, recv_sem=rsem,
            device_id=device, device_id_type=MESH)

    copies = [pltpu.make_async_copy(src, dst, local_sem.at[i]) for i, (src, dst) in enumerate((
        (counts_hbm, counts_ref), (partners_hbm, partners_ref), (modes_hbm, modes_ref),
        (inverse_hbm.at[:, 0], inverse_raw), (load_hbm, y_ref),
        (dirichlet_hbm, weights.at[0]), (dual_hbm, weights.at[1])))]
    for c in copies:
        c.start()

    barrier = pltpu.get_barrier_semaphore()

    def greet(device):
        pl.semaphore_signal(barrier, inc=1, device_id=device, device_id_type=MESH)

    @pl.loop(1, depth)
    def _(i):
        greet((seat(lax.rem(layer + i, depth), column, core), b))

    @pl.loop(1, width)
    def _(i):
        greet((seat(layer, lax.rem(column + i, width), core), b))

    @pl.loop(0, depth)
    def _(z):
        greet((seat(z, next_column[0], 1 - core), b))
        greet((seat(z, next_column[1], 1 - core), b))

    for f in (2, 3):
        @pl.when(exists[f])
        def _(f=f):
            for i in range(1, depth):
                greet((seat(lax.rem(layer + i, depth), column, core), neighbours[f][1]))

    @pl.loop(1, ny)
    def _(i):
        greet((a, lax.rem(b + i, ny)))

    for f in (0, 1):
        @pl.when(exists[f])
        def _(f=f):
            for i in range(1, height):
                greet((neighbours[f][0], far * height + lax.rem(rise + i, height)))

    mode_send[...] = jnp.zeros_like(mode_send)
    copies[2].wait()
    wide = modes_ref[...].astype(F32)
    for f in range(4):
        mode_send[f, 0:modes, 0:face] = wide[:, f * face:(f + 1) * face]
    count = [e.astype(jnp.int32) for e in exists]
    pl.semaphore_wait(
        barrier, depth - 1 + width - 1 + 2 * depth + ny - 1
        + (depth - 1) * (count[2] + count[3]) + (height - 1) * (count[0] + count[1]))

    def mode_copy(f, g):
        return remote(mode_send.at[f], mode_recv.at[g], mode_ssem.at[f], mode_rsem.at[g], neighbours[f])

    for f in range(4):
        @pl.when(exists[f])
        def _(f=f):
            mode_copy(f, f ^ 1).start()

    face_send[...] = jnp.zeros_like(face_send)
    part_send[...] = jnp.zeros_like(part_send)
    partial[...] = jnp.zeros_like(partial)
    copies[0].wait()
    copies[1].wait()
    position = lax.broadcasted_iota(jnp.int32, (1, face), 1)
    slot = jnp.concatenate([
        jnp.where(position < counts_ref[:, f:f + 1], partners_ref[f:f + 1, :] + f * face_pad, -1)
        for f in range(4)], axis=1)
    live = (slot >= 0).astype(F32)
    for f in range(4):
        rows = lax.broadcasted_iota(jnp.int32, (face_pad, slots), 0) + f * face_pad
        pick[f] = (rows == slot).astype(F32).astype(BF16)
    own_modes = jnp.concatenate([wide * live, jnp.zeros((padded - modes, slots), F32)], axis=0)
    mode_ext[0:padded, :] = own_modes.astype(BF16)

    copies[3].wait()
    raw_high, raw_low = halves(inverse_raw[...])
    out_row = lax.broadcasted_iota(jnp.int32, (ny * padded, ny * modes), 0)
    in_row = lax.broadcasted_iota(jnp.int32, (ny * padded, ny * modes), 1)
    place = lax.bitwise_and(out_row, padded - 1)
    row_pick = ((lax.shift_right_logical(out_row, 4) * modes + place == in_row) & (place < modes))
    row_pick = row_pick.astype(F32).astype(BF16)
    raw_high = mm(row_pick, raw_high).astype(BF16)
    raw_low = mm(row_pick, raw_low).astype(BF16)
    for p in range(2):
        in_col = lax.broadcasted_iota(jnp.int32, (nx * modes, chips * padded), 0)
        out_col = lax.broadcasted_iota(jnp.int32, (nx * modes, chips * padded), 1)
        place = lax.bitwise_and(out_col, padded - 1)
        group = lax.shift_right_logical(out_col, 4)
        source = (2 * group + p) * modes + place
        col_pick = ((source == in_col) & (place < modes)).astype(F32).astype(BF16)
        inv_high[p] = mm(raw_high, col_pick).astype(BF16)
        inv_low[p] = mm(raw_low, col_pick).astype(BF16)

    for f in range(4):
        @pl.when(exists[f])
        def _(f=f):
            mode_copy(f, f).wait_recv()
        given = jnp.where(exists[f], mode_recv[f], 0.0).astype(BF16)
        mode_ext[(f + 1) * padded:(f + 2) * padded, :] = mm(given, pick[f]).astype(BF16)

    for f in range(4):
        @pl.when(exists[f])
        def _(f=f):
            mode_copy(f, f ^ 1).wait_send()

    packed = modes * loads // lanes

    def share(parts):
        blank = jnp.zeros((5 * padded, lanes - loads), F32)
        wide = wrap_rows(jnp.concatenate([parts, blank], axis=1), loads, packed)
        part_send[...] = wide.reshape(5, padded, lanes)

    copies[4].wait()
    high, low = halves(y_ref[...])
    share(dot_nt(mode_ext[...], high) + dot_nt(mode_ext[...], low))

    spare = lanes - loads
    lane = lax.broadcasted_iota(jnp.int32, (padded, lanes), 1)
    wide_lane = lax.broadcasted_iota(jnp.int32, (width * padded, lanes), 1)
    used_row = lax.broadcasted_iota(jnp.int32, (padded, lanes), 0) < modes
    chebyshev = chebyshev_coefficients()

    def body(r, carry):
        def face_copy(f, g):
            return remote(face_send.at[f], face_recv.at[r, g],
                          face_ssem.at[f], face_rsem.at[r, g], neighbours[f])

        def near_copy(f, spot, device):
            return remote(part_send.at[f, 0:packed], near_recv.at[r, spot, f if f == 0 else ((f - 1) ^ 1) + 1, 0:packed],
                          near_ssem.at[f], near_rsem.at[r, f if f == 0 else ((f - 1) ^ 1) + 1], device)

        def near_block(kind, n):
            block = near_recv.at[r, 0:n, kind, 0:packed]
            return remote(block, block, near_ssem.at[kind], near_rsem.at[r, kind], (partner, b))

        def gather_copy(block, device):
            return remote(block, block, gather_ssem, gather_rsem.at[r], device)

        def relay_copy(p):
            block = gathered.at[r, p, :, :, 0:modes]
            return remote(block, block, relay_ssem, relay_rsem.at[r], (partner, b))

        def across_copy(src, dst, device):
            return remote(src, dst, across_ssem, across_rsem.at[r], device)

        def along_copy(src, dst, device):
            return remote(src, dst, along_ssem, along_rsem.at[r], device)

        def side_copy(src, dst, side, device):
            return remote(src, dst, side_ssem.at[side], side_rsem.at[r, 1 - side], device)

        def side_block(side):
            block = side_recv.at[r, side, :, 0:packed]
            return remote(block, block, side_ssem.at[side], side_rsem.at[r, side], (partner, b))

        for f in (3, 2):
            @pl.when(exists[f])
            def _(f=f):
                for i in range(depth):
                    device = (seat(lax.rem(layer + i, depth), column, core), neighbours[f][1])
                    near_copy(f + 1, layer, device).start()
        for f in (0, 1):
            @pl.when(exists[f])
            def _(f=f):
                spot = lax.div(lax.div(neighbours[f][0], 2), width)
                for z in range(depth):
                    near_copy(f + 1, spot, (seat(z, next_column[f], 1 - core), b)).start()
        for i in range(1, depth):
            near_copy(0, layer, (seat(lax.rem(layer + i, depth), column, core), b)).start()
        @pl.when(r == 0)
        def _():
            copies[5].wait()
            copies[6].wait()
            for which in range(2):
                high, low = halves(dot_nt(mode_ext[...], weights[which]))
                dm_high[which] = high
                dm_low[which] = low

        @pl.when(r > 0)
        def _():
            y_ref[...] = mm(x_ref[...], weights[lax.rem(r + 1, 2)])

        y = y_ref[...]
        for f in range(4):
            face_send[f, :, 0:face] = y[:, f * face:(f + 1) * face]

        first = (column == 0) & (core == 0)
        final = (column == width - 1) & (core == 1)
        near_block(0, depth - 1).wait_recv()
        for kind, edge in ((1, first), (2, final)):
            @pl.when(edge)
            def _(kind=kind):
                near_block(kind, depth - 1).wait_recv()

            @pl.when(jnp.logical_not(edge))
            def _(kind=kind):
                near_block(kind, depth).wait_recv()
        for f in (2, 3):
            @pl.when(exists[f])
            def _(f=f):
                near_block(f + 1, depth).wait_recv()
        sums = []
        for z in range(depth):
            coeffs = jnp.where(layer == z, part_send[0], near_recv[r, z, 0])
            west, east = near_recv[r, z, 1], near_recv[r, z, 2]
            if z == 0:
                west = jnp.where(first, 0.0, west)
            if z == depth - 1:
                east = jnp.where(final, 0.0, east)
            coeffs = coeffs + (west + east)
            for f in (2, 3):
                coeffs = coeffs + jnp.where(exists[f], near_recv[r, z, f + 1], 0.0)
            sums.append(unwrap_rows(coeffs, loads, packed))
        for z in range(depth - 1):
            tail = pltpu.roll(sums[-1], loads - spare * z, 1)
            gathered[r, core, z, column] = jnp.where(lane < loads, sums[z], tail)
        mine = gathered.at[r, core, :, column, 0:modes]
        for i in steps:
            gather_copy(mine, (seat(layer, lax.rem(column + i, width), core), b)).start()

        for f in range(4):
            @pl.when(exists[f])
            def _(f=f):
                face_copy(f, f ^ 1).start()

        others = gathered.at[r, core, :, 0:width - 1, 0:modes]
        gather_copy(others, (partner, b)).wait_recv()
        relay_copy(core).start()

        def coarse(p):
            heads = [jnp.where(used_row[None], gathered[r, p, z], 0.0).reshape(width * padded, lanes)
                     for z in range(depth - 1)]
            last = pltpu.roll(heads[-1], lanes - spare, 1)
            for z in reversed(range(depth - 2)):
                last = jnp.where(wide_lane < spare * (z + 1), pltpu.roll(heads[z], spare * (z + 1), 1), last)
            values = jnp.concatenate(heads + [last], axis=0)
            high, low = halves(values)
            return mm(inv_high[p], high) + mm(inv_high[p], low) + mm(inv_low[p], high)

        half = coarse(core)
        relay_copy(1 - core).wait_recv()
        outcome = wrap_rows(half + coarse(1 - core), loads, packed)
        partial[1:ny + 1] = outcome.reshape(ny, padded, lanes)

        for i in range(1, length):
            other = lax.rem(far + i, length)
            across_copy(partial.at[pl.ds(height * other, height + 2), 0:packed],
                        across_recv.at[r, far, :, 0:packed], (a, other * height + rise)).start()
        across_all = across_recv.at[r, 0:length - 1, :, 0:packed]
        across_copy(across_all, across_all, (partner, b)).wait_recv()
        total = partial[pl.ds(height * far, height + 2)]
        for x in range(length):
            total = total + jnp.where(far == x, 0.0, across_recv[r, x])
        summed[...] = total
        for i in range(1, height):
            other = lax.rem(rise + i, height)
            along_copy(summed.at[pl.ds(other, 3), 0:packed], along_recv.at[r, rise, :, 0:packed],
                       (a, far * height + other)).start()
        for side in range(2):
            @pl.when(exists[side])
            def _(side=side):
                for i in range(height):
                    other = lax.rem(rise + height - i, height)
                    side_copy(summed.at[other + 1, 0:packed], side_recv.at[r, 1 - side, rise, 0:packed],
                              side, (neighbours[side][0], far * height + other)).start()

        matched = live * y
        for f in range(4):
            @pl.when(exists[f])
            def _(f=f):
                face_copy(f, f).wait_recv()
            for piece in thirds(jnp.where(exists[f], face_recv[r, f], 0.0)):
                matched = matched + mm(piece, pick[f])
        v_ref[...] = matched

        along_all = along_recv.at[r, 0:height - 1, :, 0:packed]
        along_copy(along_all, along_all, (partner, b)).wait_recv()
        trio = summed[pl.ds(rise, 3)]
        for z in range(height):
            trio = trio + jnp.where(rise == z, 0.0, along_recv[r, z])
        sides = []
        for side in range(2):
            @pl.when(exists[side])
            def _(side=side):
                side_block(side).wait_recv()
            sides.append(sum(side_recv[r, side, z] for z in range(height)))
        blocks = [trio[1]]
        for f, block in enumerate((sides[0], sides[1], trio[0], trio[2])):
            blocks.append(jnp.where(exists[f], block, 0.0))
        full = unwrap_rows(jnp.concatenate(blocks, axis=0), loads, packed)
        high, low = halves(full)
        correction = dot_tn(high, mode_ext[...]) + dot_tn(low, mode_ext[...])
        out = v_ref[...] - correction[0:loads]

        for f in range(4):
            @pl.when(exists[f])
            def _(f=f):
                near_block(f + 1, depth).wait_send()
                face_copy(f, f ^ 1).wait_send()
        for side in range(2):
            @pl.when(exists[side])
            def _(side=side):
                side_block(side).wait_send()
        near_block(0, depth - 1).wait_send()
        gather_copy(others, (partner, b)).wait_send()
        relay_copy(core).wait_send()
        across_copy(across_all, across_all, (partner, b)).wait_send()
        along_copy(along_all, along_all, (partner, b)).wait_send()

        def advance(vector, which):
            x = vector.astype(BF16)
            share(dot_nt(dm_high[which], x) + dot_nt(dm_low[which], x))
            x_ref[...] = x

        @pl.when(r == 0)
        def _():
            res_ref[...] = out
            advance(out, 0)

        @pl.when(r == 1)
        def _():
            step = chebyshev[0][0] * out
            mult_ref[...] = step
            advance(step, 1)

        @pl.when(r == 2)
        def _():
            rest = res_ref[...] - out
            res_ref[...] = rest
            advance(rest, 0)

        @pl.when(r == 3)
        def _():
            step = chebyshev[1][0] * out + chebyshev[1][1] * mult_ref[...]
            step_ref[...] = step
            advance(step, 1)

        @pl.when(r == 4)
        def _():
            last_ref[...] = out

        return carry

    lax.fori_loop(0, ROUNDS, body, 0)


def local(nx, ny, load, dual_operator, dirichlet, modes, coarse_inverse, face_counts, partners):
    loads, slots = load.shape[2:]
    count = modes.shape[2]
    face = slots // 4
    face_pad = -(-face // 128) * 128
    padded = 16
    lanes = 128
    depth = 4
    width = nx // 2 // depth
    height = 3 if ny % 3 == 0 else 2
    vmem = pl.BlockSpec(memory_space=pltpu.VMEM)
    hbm = pl.BlockSpec(memory_space=pltpu.HBM)
    dma = pltpu.SemaphoreType.DMA
    first, second, before, last = pl.pallas_call(
        functools.partial(kernel, nx, ny),
        out_shape=(jax.ShapeDtypeStruct((loads, slots), F32),) * 4,
        in_specs=[hbm] * 7,
        out_specs=(vmem,) * 4,
        scratch_shapes=[
            pltpu.VMEM((1, 4), jnp.int32),
            pltpu.VMEM((4, face), jnp.int32),
            pltpu.VMEM((count, slots), BF16),
            pltpu.VMEM((loads, slots), BF16),
            pltpu.VMEM((2, 5 * padded, slots), BF16),
            pltpu.VMEM((2, 5 * padded, slots), BF16),
            pltpu.VMEM((2, slots, slots), BF16),
            pltpu.VMEM((ny * count, nx * count), F32),
            pltpu.VMEM((4, face_pad, slots), BF16),
            pltpu.VMEM((5 * padded, slots), BF16),
            pltpu.VMEM((4, padded, face_pad), F32),
            pltpu.VMEM((4, padded, face_pad), F32),
            pltpu.VMEM((loads, slots), F32),
            pltpu.VMEM((loads, slots), F32),
            pltpu.VMEM((2, ny * padded, nx // 2 * padded), BF16),
            pltpu.VMEM((2, ny * padded, nx // 2 * padded), BF16),
            pltpu.VMEM((4, loads, face_pad), F32),
            pltpu.VMEM((ROUNDS, 4, loads, face_pad), F32),
            pltpu.VMEM((5, padded, lanes), F32),
            pltpu.VMEM((ROUNDS, depth, 5, padded, lanes), F32),
            pltpu.VMEM((ROUNDS, 2, depth - 1, width, padded, lanes), F32),
            pltpu.VMEM((ny + 2, padded, lanes), F32),
            pltpu.VMEM((ROUNDS, ny // height, height + 2, padded, lanes), F32),
            pltpu.VMEM((height + 2, padded, lanes), F32),
            pltpu.VMEM((ROUNDS, height, 3, padded, lanes), F32),
            pltpu.VMEM((ROUNDS, 2, height, padded, lanes), F32),
            dma((7,)), dma((4,)), dma((4,)), dma((4,)), dma((ROUNDS, 4)), dma((5,)), dma((ROUNDS, 5)),
            dma, dma((ROUNDS,)), dma, dma((ROUNDS,)),
            dma, dma((ROUNDS,)), dma, dma((ROUNDS,)), dma((2,)), dma((ROUNDS, 2)),
        ],
        compiler_params=pltpu.CompilerParams(
            collective_id=0, has_side_effects=True, vmem_limit_bytes=40 * 1024 * 1024),
    )(*(pltpu.with_memory_space_constraint(x, pltpu.HBM) for x in (
        face_counts[0], partners[0, 0], load[0, 0], modes[0, 0],
        dual_operator[0, 0], dirichlet[0, 0], coarse_inverse[0])))
    return (first + second)[None, None], (before - last)[None, None]


def solution(mesh):
    nx, ny = mesh.shape["gx"], mesh.shape["gy"]
    return jax.shard_map(
        functools.partial(local, nx, ny),
        mesh=mesh,
        in_specs=(
            P("gx", "gy", None, None),
            P("gx", "gy", None, None),
            P("gx", "gy", None, None),
            P("gx", "gy", None, None),
            P("gx", None, "gy", None),
            P("gx", "gy", None),
            P("gx", "gy", None, None),
        ),
        out_specs=(P("gx", "gy", None, None), P("gx", "gy", None, None)),
        check_vma=False,
    )
```

time: 188 us -> 151 us (0.80); the launches traced: 186 us -> 151 us
  Pallas kernels: 178 us -> 149 us
  local copies, waits for them, and re-layouts: 6.29 us -> 0 us
    pallas_call x1, Pallas kernels: 178 us -> 149 us  [local(): pl.pallas_call(functools.partial(kernel, nx, ny), out_shape=(jax.ShapeDty...]
    unnamed x3 -> x0, local copies, waits for them, and re-layouts: 5.27 us -> none
where the time goes in v2:
time: 151 us
  Pallas kernels  149 us (99%)
    pallas_call x1, Pallas kernels, local(): pl.pallas_call(functools.partial(kernel, nx, ny), out_shape=(jax.ShapeDty...  149 us

profile of v2, /device:TPU:1, one launch (start us, length us, event | category | flops | bytes accessed | tf_op | source)
XLA Modules:
  0.0 151.0 jit_solution(14394141555335855527)
XLA Ops:
  0.6 149.4 %shard_map.86 = (f32[96,896]{1,0:T(8,128)S(1)}, f32[96,896]{1,0:T(8,128)S(1)}, f32[96,896]{1,0:T(8,128)S(1)}, f32[96,896]{1,0:T(8,128)S(1)}) custom-call(s32[1,4]{1,0:T(1,128)} %bitcast.17, s32[4,224]{1,0:T(4,128)} %bitcast.16, f32[96,896]{1,0:T(8,128)} %bitcast.14, bf16[12,896]{1,0:T(8,128)(2,1)} %bitcast.15, bf16[896,896]{1,0:T(8,128)(2,1)} %bitcast.11, ...), custom_call_target="tpu_custom_call" | custom-call | tf_op jit(solution)/shard_map/pallas_call | solution.py:482
  150.0 0.9 subtract_bitcast_fusion
